TPU v7x, 32 devices: a whole 2x2x4 slice. The times are simulated.
32 devices in a mesh: space: 8 (over z, y), segment: 4 (over x, core).
Axes of the slice: x: 2, y: 2, z: 4, core: 2. Of those that a mesh axis runs over, the one named last changes fastest.
Arguments:
- saved_inputs: bfloat16 [4, 1048576], P('segment', 'space'), may hold values from -5.5 to 5.5
- conv_weights: bfloat16 [4, 221184], P('segment'), may hold values from -0.4375 to 0.4375
- top_gradient: bfloat16 [128, 8, 2, 32], P(None, 'space'), may hold values from -6 to 6
Outputs:
- weight_grads: float32 [4, 221184], P('segment')
All inputs are finite; a program needn't handle non-finite values.
Results may differ from a plain program's by a relative error of at most 0.0023.
Values may be sent and summed in bfloat16 or wider, within the bound.
No kernel may reach another device: no remote copies, remote signals or barrier semaphores. Data moves between devices by JAX's collectives and lax.ppermute only.
A program may use at most 64 MiB of HBM per device.

v0:
```python
import math
import jax
import jax.numpy as jnp
from jax import lax
from jax.sharding import PartitionSpec as P

C0 = 4
C1 = 16
C2 = 32
C3 = 64
C4 = 128
CZ = 4
CY = 8
CX = 128
slope_negative = 0.3
tap_offsets = [
    (tap_z, tap_y, tap_x) for tap_z in range(3) for tap_y in range(3) for tap_x in range(3)
]
parity_terms = [(0, 0, 0), (0, 2, -1), (1, 1, 0)]


def as_sent(x):

    def short(part):
        return part.astype(jnp.bfloat16) if part.dtype == jnp.float32 else part

    return jax.tree.map(short, x)


def with_halo(cells, sides, width):
    for axis, dim in sides:
        count = lax.axis_size(axis)
        ends = count - 1
        head = lax.slice_in_dim(cells, 0, width, axis=dim)
        tail = lax.slice_in_dim(cells, cells.shape[dim] - width, cells.shape[dim], axis=dim)
        cells = jnp.concatenate(
            [
                lax.ppermute(tail, axis, [(i, (i + 1) % count) for i in range(ends)]),
                cells,
                lax.ppermute(head, axis, [((i + 1) % count, i) for i in range(ends)]),
            ],
            axis=dim,
        )
    return cells


def passed_along(block, axis, distance):
    devices = range(lax.axis_size(axis))
    route = [(i - distance, i) for i in devices if i - distance in devices]
    return lax.ppermute(block, axis, route)


def section_table():
    return [
        (C0, C1, 1, CZ, CY, CX),
        (C1, C2, 1, CZ, CY, CX),
        (C2, C3, 2, CZ, CY, CX),
        (C3, C4, 2, CZ // 2, CY // 2, CX // 2),
    ]


def extend_fine(volume):
    return with_halo(as_sent(volume), (("space", 1),), 1).astype(volume.dtype)


def send_back(message):
    return jax.tree.map(
        lambda part, own: part.astype(own.dtype),
        passed_along(as_sent(message), "segment", -1),
        message,
    )


def pad_cross(volume, low_side, high_side):
    return jnp.pad(volume, ((0, 0), (0, 0), (low_side, high_side), (low_side, high_side)))


def fine_weight_grad(act_ext, upstream):
    padded = pad_cross(act_ext, 1, 1)
    out_z, out_y, out_x = (upstream.shape[1], upstream.shape[2], upstream.shape[3])
    results = []
    for tap_z, tap_y, tap_x in tap_offsets:
        window = padded[:, tap_z : tap_z + out_z, tap_y : tap_y + out_y, tap_x : tap_x + out_x]
        results.append(
            jnp.einsum("dzyx,czyx->dc", upstream, window, preferred_element_type=jnp.float32)
        )
    return jnp.stack(results)


def coarse_weight_grad(act_ext, upstream):
    padded = pad_cross(act_ext, 0, 1)
    out_z, out_y, out_x = (upstream.shape[1], upstream.shape[2], upstream.shape[3])
    results = []
    for tap_z, tap_y, tap_x in tap_offsets:
        window = padded[
            :,
            tap_z : tap_z + 2 * out_z : 2,
            tap_y : tap_y + 2 * out_y : 2,
            tap_x : tap_x + 2 * out_x : 2,
        ]
        results.append(
            jnp.einsum("dzyx,czyx->dc", upstream, window, preferred_element_type=jnp.float32)
        )
    return jnp.stack(results)


def fine_input_grad(weights, delta_ext):
    padded = pad_cross(delta_ext, 1, 1)
    size_z, size_y, size_x = (delta_ext.shape[1] - 2, delta_ext.shape[2], delta_ext.shape[3])
    summed = jnp.zeros((weights.shape[2], size_z, size_y, size_x), jnp.float32)
    for position, (tap_z, tap_y, tap_x) in enumerate(tap_offsets):
        window = padded[
            :,
            2 - tap_z : 2 - tap_z + size_z,
            2 - tap_y : 2 - tap_y + size_y,
            2 - tap_x : 2 - tap_x + size_x,
        ]
        summed = summed + jnp.einsum(
            "dc,dzyx->czyx", weights[position], window, preferred_element_type=jnp.float32
        )
    return summed


def coarse_input_grad(weights, delta_ext):
    padded = pad_cross(delta_ext, 1, 0)
    out_z, out_y, out_x = (delta_ext.shape[1] - 1, delta_ext.shape[2], delta_ext.shape[3])
    parity_sums = {}
    for rest_z, tap_z, step_z in parity_terms:
        for rest_y, tap_y, step_y in parity_terms:
            for rest_x, tap_x, step_x in parity_terms:
                window = padded[
                    :,
                    1 + step_z : 1 + step_z + out_z,
                    1 + step_y : 1 + step_y + out_y,
                    1 + step_x : 1 + step_x + out_x,
                ]
                contribution = jnp.einsum(
                    "dc,dzyx->czyx",
                    weights[9 * tap_z + 3 * tap_y + tap_x],
                    window,
                    preferred_element_type=jnp.float32,
                )
                parity = (rest_z, rest_y, rest_x)
                parity_sums[parity] = (
                    parity_sums[parity] + contribution if parity in parity_sums else contribution
                )
    stacked = jnp.stack(
        [
            jnp.stack(
                [
                    jnp.stack([parity_sums[rest_z, rest_y, rest_x] for rest_x in (0, 1)])
                    for rest_y in (0, 1)
                ]
            )
            for rest_z in (0, 1)
        ]
    )
    channels = weights.shape[2]
    return jnp.transpose(stacked, (3, 4, 0, 5, 1, 6, 2)).reshape(
        channels, 2 * out_z, 2 * out_y, 2 * out_x
    )


def weight_term(act_ext, upstream, stride_size, scale_factor):
    if stride_size == 1:
        return fine_weight_grad(act_ext, upstream) * scale_factor
    return coarse_weight_grad(act_ext, upstream) * scale_factor


def message_term(weights, delta_ext, activation, stride_size):
    if stride_size == 1:
        backward = fine_input_grad(weights, delta_ext)
    else:
        backward = coarse_input_grad(weights, delta_ext)
    return (backward * jnp.where(activation > 0, 1.0, slope_negative)).astype(jnp.bfloat16)


def shards(saved_inputs, conv_weights, top_gradient):
    segment_index = lax.axis_index("segment")
    space_count = lax.axis_size("space")
    own_row = saved_inputs[0]
    own_weights = conv_weights[0]
    weight_room = conv_weights.shape[1]
    upstream = top_gradient
    collected = jnp.zeros((weight_room,), jnp.float32)
    for section in (3, 2, 1, 0):
        chan_in, chan_out, stride_size, depth_cells, height, breadth = section_table()[section]
        activation = own_row[: chan_in * depth_cells * height * breadth].reshape(
            chan_in, depth_cells, height, breadth
        )
        weights = own_weights[: 27 * chan_out * chan_in].reshape(27, chan_out, chan_in)
        active = segment_index == section
        scale_factor = 1.0 / math.sqrt(
            space_count * upstream.shape[1] * upstream.shape[2] * upstream.shape[3]
        )
        if stride_size == 1:
            if section > 0:
                joined = extend_fine(jnp.concatenate([activation, upstream], 0))
                act_ext = joined[:chan_in]
                delta_ext = joined[chan_in:]
            else:
                act_ext = extend_fine(activation)
                delta_ext = upstream
        else:
            upper_plane = passed_along(activation[:, :1], "space", -1)
            lower_plane = passed_along(as_sent(upstream[:, -1:]), "space", 1)
            act_ext = jnp.concatenate([activation, upper_plane], 1)
            delta_ext = jnp.concatenate([lower_plane, upstream], 1)
        grad_shape = (27, chan_out, chan_in)
        message_shape = activation.shape

        def weight_branch(act_ext, upstream, stride_size=stride_size, scale_factor=scale_factor):
            return weight_term(act_ext, upstream, stride_size, scale_factor)

        def weight_skip(act_ext, upstream, grad_shape=grad_shape):
            return jnp.zeros(grad_shape, jnp.float32)

        def both_branch(
            weights,
            delta_ext,
            activation,
            act_ext,
            upstream,
            stride_size=stride_size,
            scale_factor=scale_factor,
        ):
            return (
                weight_term(act_ext, upstream, stride_size, scale_factor),
                message_term(weights, delta_ext, activation, stride_size),
            )

        def both_skip(
            weights,
            delta_ext,
            activation,
            act_ext,
            upstream,
            grad_shape=grad_shape,
            message_shape=message_shape,
        ):
            return (jnp.zeros(grad_shape, jnp.float32), jnp.zeros(message_shape, jnp.bfloat16))

        if section > 0:
            local_grad, message = lax.cond(
                active, both_branch, both_skip, weights, delta_ext, activation, act_ext, upstream
            )
            passed = send_back(message)
        else:
            local_grad = lax.cond(active, weight_branch, weight_skip, act_ext, upstream)
        local_grad = lax.psum(local_grad, "space")
        flat_grad = local_grad.reshape(-1)
        collected = jnp.where(
            active, jnp.pad(flat_grad, (0, weight_room - flat_grad.shape[0])), collected
        )
        if section > 0:
            upstream = passed
    return collected[None]


def solution(mesh):
    return jax.shard_map(
        shards,
        mesh=mesh,
        in_specs=(P("segment", "space"), P("segment", None), P(None, "space", None, None)),
        out_specs=P("segment", None),
        check_vma=False,
    )
```

profile of v0, /device:TPU:0, one launch (start us, length us, event | category | flops | bytes accessed | tf_op | source)
XLA Modules:
  0.0 222.7 jit_solution(12516245438822264180)
XLA Ops:
  6.5 4.9 %collective-permute-start.4 = (bf16[128,1,2,32]{0,3,2,1:T(8,128)(2,1)}, bf16[128,1,2,32]{0,3,2,1:T(8,128)(2,1)S(1)}, u32[]{:S(2)}, u32[]{:S(2)}) collective-permute-start(bf16[128,1,2,32]{0,3,2,1:T(8,128)(2,1)} %param.13), channel_id=1, source_target_pairs={{0,4},{4,8},{8,12},{12,16},{16,20},{20,24},{24,28},{1,5},{5,9},{9,... | collective-permute-start | bytes 49160 | tf_op jit(solution)/shard_map/ppermute | solution.py:50
  11.4 1.3 slice_reduce_fusion.82
  12.8 1.3 collective-permute-start.3
  14.9 4.1 %collective-permute-done.3 = bf16[64,1,4,64]{3,2,1,0:T(4,128)(2,1)S(1)} collective-permute-done((bf16[64,1,4,64]{3,2,1,0:T(4,128)(2,1)S(1)}, bf16[64,1,4,64]{3,2,1,0:T(4,128)(2,1)S(1)}, u32[]{:S(2)}, u32[]{:S(2)}) %collective-permute-start.3) | collective-permute-done | bytes 32800 | tf_op jit(solution)/shard_map/ppermute | solution.py:50
  19.9 0.9 copy-done.1
  20.9 1.0 copy.205
  21.9 1.3 collective-permute-start.5
  23.2 1.6 reduce.83
  24.8 1.3 collective-permute-start.2
  26.1 5.0 %collective-permute-start.6 = (bf16[64,1,4,64]{3,0,2,1:T(8,128)(2,1)S(1)}, bf16[64,1,4,64]{3,0,2,1:T(8,128)(2,1)S(1)}, u32[]{:S(2)}, u32[]{:S(2)}) collective-permute-start(bf16[64,1,4,64]{3,0,2,1:T(8,128)(2,1)S(1)} %copy.463), channel_id=1, source_target_pairs={{0,4},{4,8},{8,12},{12,16},{16,20},{20,24},{24,28},{1,5},{5,9},{9,... | collective-permute-start | bytes 98312 | tf_op jit(solution)/shard_map/ppermute | solution.py:50
  32.5 1.4 collective-permute-done.6
  33.9 2.1 conditional.5
  33.9 1.2 broadcast.41
  35.2 0.8 broadcast.40
  36.0 1.6 copy.210
  37.6 1.3 collective-permute-start.7
  38.9 1.7 slice_reduce_fusion.81
  40.6 1.3 copy.217
  41.9 0.9 reshape.416
  43.0 4.4 %collective-permute-start.8 = (bf16[48,1,8,128]{3,0,1,2:T(8,128)(2,1)S(1)}, bf16[48,1,8,128]{3,0,1,2:T(8,128)(2,1)S(1)}, u32[]{:S(2)}, u32[]{:S(2)}) collective-permute-start(bf16[48,1,8,128]{3,0,1,2:T(8,128)(2,1)S(1)} %get-tuple-element.206), channel_id=1, source_target_pairs={{0,4},{4,8},{8,12},{12,16},{16,20},{20,24},{24,28},{1,5},{5,9},{9,... | collective-permute-start | bytes 294920 | tf_op jit(solution)/shard_map/ppermute | solution.py:38
  47.4 1.3 collective-permute-start.9
  48.7 1.0 slice_reduce_fusion.83
  49.8 5.5 %collective-permute-done.9 = bf16[48,1,8,128]{3,0,1,2:T(8,128)(2,1)S(1)} collective-permute-done((bf16[48,1,8,128]{3,0,1,2:T(8,128)(2,1)S(1)}, bf16[48,1,8,128]{3,0,1,2:T(8,128)(2,1)S(1)}, u32[]{:S(2)}, u32[]{:S(2)}) %collective-permute-start.9) | collective-permute-done | bytes 98336 | tf_op jit(solution)/shard_map/ppermute | solution.py:40
  55.7 1.3 collective-permute-start.10
  57.0 4.8 %collective-permute-start = (bf16[4,1,8,128]{3,2,1,0:T(8,128)(2,1)S(1)}, bf16[4,1,8,128]{3,2,1,0:T(8,128)(2,1)S(1)}, u32[]{:S(2)}, u32[]{:S(2)}) collective-permute-start(bf16[4,1,8,128]{3,2,1,0:T(8,128)(2,1)S(1)} %get-tuple-element.208), channel_id=1, source_target_pairs={{0,4},{4,8},{8,12},{12,16},{16,20},{20,24},{24,28},{1,5},{5,9},{9,... | collective-permute-start | bytes 24584 | tf_op jit(solution)/shard_map/ppermute | solution.py:38
  61.8 1.3 collective-permute-start.1
  63.2 4.2 %collective-permute-done.1 = bf16[4,1,8,128]{3,2,1,0:T(8,128)(2,1)S(1)} collective-permute-done((bf16[4,1,8,128]{3,2,1,0:T(8,128)(2,1)S(1)}, bf16[4,1,8,128]{3,2,1,0:T(8,128)(2,1)S(1)}, u32[]{:S(2)}, u32[]{:S(2)}) %collective-permute-start.1) | collective-permute-done | bytes 8224 | tf_op jit(solution)/shard_map/ppermute | solution.py:40
  67.8 98.1 %collective-permute-done.10 = bf16[16,4,8,128]{3,0,1,2:T(8,128)(2,1)S(1)} collective-permute-done((bf16[16,4,8,128]{3,0,1,2:T(8,128)(2,1)S(1)}, bf16[16,4,8,128]{3,0,1,2:T(8,128)(2,1)S(1)}, u32[]{:S(2)}, u32[]{:S(2)}) %collective-permute-start.10) | collective-permute-done | bytes 131104 | tf_op jit(solution)/shard_map/ppermute | solution.py:50
  165.8 6.0 %conditional.7 = (f32[27,16,4]{1,2,0:T(4,128)S(1)}) conditional(s32[]{:T(128)} %convert_element_type.41, () %tuple.35, (bf16[4,6,8,128]{3,2,1,0:T(8,128)(2,1)S(1)}, bf16[16,4,8,128]{3,0,1,2:T(8,128)(2,1)S(1)}) %tuple.42), branch_computations={%region_6.7_spmd, %region_7.8_spmd} | conditional | flops 14157503 | bytes 4984328 | solution.py:249
  172.2 37.4 %all-reduce.10 = (f32[13824]{0:T(1024)S(1)}, f32[1728]{0:T(1024)S(1)}) all-reduce(f32[13824]{0:T(1024)S(1)} %reshape.415, f32[1728]{0:T(1024)S(1)} %reshape.414), channel_id=1, replica_groups=mesh['space'=8,'segment'=4] {'space'}, use_global_device_ids=true, to_apply=%region_9.10 | all-reduce | flops 15552 | bytes 124416 | tf_op jit(solution)/shard_map/psum | solution.py:250
  209.6 4.2 %all-reduce.14.cloned.1.call-done = (f32[27,128,64]{1,2,0:T(8,128)}, f32[55296]{0:T(1024)}) async-done(((f32[27,128,64]{1,2,0:T(8,128)}, f32[55296]{0:T(1024)}), (f32[27,128,64]{1,2,0:T(8,128)}, f32[55296]{0:T(1024)})) %all-reduce.14.cloned.1.call-update) | async-done | bytes 1105936 | tf_op jit(solution)/shard_map/psum | solution.py:250
  214.8 1.0 select_select_fusion
  (71 shorter events, 12.3 us)
Async XLA Ops:
  6.5 207.3 %all-reduce.14.cloned.1.call-start = ((), (), s32[]{:S(2)}) async-start(), calls=%async_computation | async-start | bytes 2211840 | tf_op jit(solution)/shard_map/psum | solution.py:250
  6.5 7.6 %collective-permute-start.4 = (bf16[128,1,2,32]{0,3,2,1:T(8,128)(2,1)}, bf16[128,1,2,32]{0,3,2,1:T(8,128)(2,1)S(1)}, u32[]{:S(2)}, u32[]{:S(2)}) collective-permute-start(bf16[128,1,2,32]{0,3,2,1:T(8,128)(2,1)} %param.13), channel_id=1, source_target_pairs={{0,4},{4,8},{8,12},{12,16},{16,20},{20,24},{24,28},{1,5},{5,9},{9,... | collective-permute-start | bytes 49160 | tf_op jit(solution)/shard_map/ppermute | solution.py:50
  12.8 6.2 %collective-permute-start.3 = (bf16[64,1,4,64]{3,2,1,0:T(4,128)(2,1)S(1)}, bf16[64,1,4,64]{3,2,1,0:T(4,128)(2,1)S(1)}, u32[]{:S(2)}, u32[]{:S(2)}) collective-permute-start(bf16[64,1,4,64]{3,2,1,0:T(4,128)(2,1)S(1)} %slice.982), channel_id=1, source_target_pairs={{4,0},{8,4},{12,8},{16,12},{20,16},{24,20},{28,24},{5,1},{9,5},{13... | collective-permute-start | bytes 98312 | tf_op jit(solution)/shard_map/ppermute | solution.py:50
  19.2 4.0 %copy-start.2 = (bf16[1,131072]{1,0:T(2,128)(2,1)S(1)}, bf16[1,131072]{1,0:T(2,128)(2,1)}, u32[]{:S(2)}) copy-start(bf16[1,131072]{1,0:T(2,128)(2,1)} %param.11) | copy-start | bytes 786436
  19.9 0.9 copy-start.1
  21.9 4.2 %collective-permute-start.5 = (bf16[64,2,4,64]{3,0,1,2:T(8,128)(2,1)S(1)}, bf16[64,2,4,64]{3,0,1,2:T(8,128)(2,1)S(1)}, u32[]{:S(2)}, u32[]{:S(2)}) collective-permute-start(bf16[64,2,4,64]{3,0,1,2:T(8,128)(2,1)S(1)} %copy.205), channel_id=1, source_target_pairs={{1,0},{2,1},{3,2},{5,4},{6,5},{7,6},{9,8},{10,9},{11,10},{13,12},{... | collective-permute-start | bytes 196616 | tf_op jit(solution)/shard_map/ppermute | solution.py:50
  24.8 6.9 %collective-permute-start.2 = (bf16[32,1,8,128]{3,2,1,0:T(8,128)(2,1)S(1)}, bf16[32,1,8,128]{3,2,1,0:T(8,128)(2,1)S(1)}, u32[]{:S(2)}, u32[]{:S(2)}) collective-permute-start(bf16[32,1,8,128]{3,2,1,0:T(8,128)(2,1)S(1)} %slice.981), channel_id=1, source_target_pairs={{4,0},{8,4},{12,8},{16,12},{20,16},{24,20},{28,24},{5,1},{9,5},{13... | collective-permute-start | bytes 196616 | tf_op jit(solution)/shard_map/ppermute | solution.py:50
  26.1 7.7 %collective-permute-start.6 = (bf16[64,1,4,64]{3,0,2,1:T(8,128)(2,1)S(1)}, bf16[64,1,4,64]{3,0,2,1:T(8,128)(2,1)S(1)}, u32[]{:S(2)}, u32[]{:S(2)}) collective-permute-start(bf16[64,1,4,64]{3,0,2,1:T(8,128)(2,1)S(1)} %copy.463), channel_id=1, source_target_pairs={{0,4},{4,8},{8,12},{12,16},{16,20},{20,24},{24,28},{1,5},{5,9},{9,... | collective-permute-start | bytes 98312 | tf_op jit(solution)/shard_map/ppermute | solution.py:50
  37.6 5.4 %collective-permute-start.7 = (bf16[32,4,8,128]{3,0,1,2:T(8,128)(2,1)S(1)}, bf16[32,4,8,128]{3,0,1,2:T(8,128)(2,1)S(1)}, u32[]{:S(2)}, u32[]{:S(2)}) collective-permute-start(bf16[32,4,8,128]{3,0,1,2:T(8,128)(2,1)S(1)} %copy.210), channel_id=1, source_target_pairs={{1,0},{2,1},{3,2},{5,4},{6,5},{7,6},{9,8},{10,9},{11,10},{13,12},{... | collective-permute-start | bytes 786440 | tf_op jit(solution)/shard_map/ppermute | solution.py:50
  43.0 6.7 %collective-permute-start.8 = (bf16[48,1,8,128]{3,0,1,2:T(8,128)(2,1)S(1)}, bf16[48,1,8,128]{3,0,1,2:T(8,128)(2,1)S(1)}, u32[]{:S(2)}, u32[]{:S(2)}) collective-permute-start(bf16[48,1,8,128]{3,0,1,2:T(8,128)(2,1)S(1)} %get-tuple-element.206), channel_id=1, source_target_pairs={{0,4},{4,8},{8,12},{12,16},{16,20},{20,24},{24,28},{1,5},{5,9},{9,... | collective-permute-start | bytes 294920 | tf_op jit(solution)/shard_map/ppermute | solution.py:38
  47.4 7.9 %collective-permute-start.9 = (bf16[48,1,8,128]{3,0,1,2:T(8,128)(2,1)S(1)}, bf16[48,1,8,128]{3,0,1,2:T(8,128)(2,1)S(1)}, u32[]{:S(2)}, u32[]{:S(2)}) collective-permute-start(bf16[48,1,8,128]{3,0,1,2:T(8,128)(2,1)S(1)} %get-tuple-element.207), channel_id=1, source_target_pairs={{4,0},{8,4},{12,8},{16,12},{20,16},{24,20},{28,24},{5,1},{9,5},{13... | collective-permute-start | bytes 294920 | tf_op jit(solution)/shard_map/ppermute | solution.py:40
  55.7 110.1 %collective-permute-start.10 = (bf16[16,4,8,128]{3,0,1,2:T(8,128)(2,1)S(1)}, bf16[16,4,8,128]{3,0,1,2:T(8,128)(2,1)S(1)}, u32[]{:S(2)}, u32[]{:S(2)}) collective-permute-start(bf16[16,4,8,128]{3,0,1,2:T(8,128)(2,1)S(1)} %copy.213), channel_id=1, source_target_pairs={{1,0},{2,1},{3,2},{5,4},{6,5},{7,6},{9,8},{10,9},{11,10},{13,12},{... | collective-permute-start | bytes 393224 | tf_op jit(solution)/shard_map/ppermute | solution.py:50
  57.0 6.2 %collective-permute-start = (bf16[4,1,8,128]{3,2,1,0:T(8,128)(2,1)S(1)}, bf16[4,1,8,128]{3,2,1,0:T(8,128)(2,1)S(1)}, u32[]{:S(2)}, u32[]{:S(2)}) collective-permute-start(bf16[4,1,8,128]{3,2,1,0:T(8,128)(2,1)S(1)} %get-tuple-element.208), channel_id=1, source_target_pairs={{0,4},{4,8},{8,12},{12,16},{16,20},{20,24},{24,28},{1,5},{5,9},{9,... | collective-permute-start | bytes 24584 | tf_op jit(solution)/shard_map/ppermute | solution.py:38
  61.8 5.5 %collective-permute-start.1 = (bf16[4,1,8,128]{3,2,1,0:T(8,128)(2,1)S(1)}, bf16[4,1,8,128]{3,2,1,0:T(8,128)(2,1)S(1)}, u32[]{:S(2)}, u32[]{:S(2)}) collective-permute-start(bf16[4,1,8,128]{3,2,1,0:T(8,128)(2,1)S(1)} %get-tuple-element.209), channel_id=1, source_target_pairs={{4,0},{8,4},{12,8},{16,12},{20,16},{24,20},{28,24},{5,1},{9,5},{13... | collective-permute-start | bytes 24584 | tf_op jit(solution)/shard_map/ppermute | solution.py:40
  213.9 0.9 copy-start.5
Sparse Core Ops, SparseCore 0:
  43.0 170.7 all-reduce.13
where the time goes:
time: 224 us; the launch traced here: 223 us
  waiting for transfers between devices  118 us (53%)
  blocking collectives  37.4 us (17%)
  starting transfers between devices  28.1 us (13%)
  local copies, waits for them, and re-layouts  14.6 us (7%)
  between operations  13.7 us (6%)
  matrix products  5.93 us (3%)
  other arithmetic  4.47 us (2%)
    ppermute x7, waiting for transfers between devices, passed_along(): return lax.ppermute(block, axis, route)  104 us
    psum x1, blocking collectives, shards(): local_grad = lax.psum(local_grad, 'space')  37.4 us
    ppermute x7, starting transfers between devices, passed_along(): return lax.ppermute(block, axis, route)  16.3 us
    ppermute x2, waiting for transfers between devices, with_halo(): lax.ppermute(head, axis, [((i + 1) % count, i) for i in range(ends)])  9.74 us
    ppermute x2, starting transfers between devices, with_halo(): lax.ppermute(tail, axis, [(i, (i + 1) % count) for i in range(ends)])  9.21 us
    dot_general x27, matrix products, fine_weight_grad(): jnp.einsum('dzyx,czyx->dc', upstream, window, preferred_element_type=jnp....  5.93 us
  transfers between devices with their start and end apart: 12, of which 7 were waited for; matrix products, arithmetic and copies ran while one was open for 7% of the time, Pallas kernels for 0%

commit v1 on v0

--- a/solution.py
+++ b/solution.py
@@ -247,7 +247,7 @@
             passed = send_back(message)
         else:
             local_grad = lax.cond(active, weight_branch, weight_skip, act_ext, upstream)
-        local_grad = lax.psum(local_grad, "space")
+        local_grad = jnp.sum(lax.all_gather(local_grad, "space"), 0)
         flat_grad = local_grad.reshape(-1)
         collected = jnp.where(
             active, jnp.pad(flat_grad, (0, weight_room - flat_grad.shape[0])), collected

time: 224 us -> 346 us (1.54)
  waiting for transfers between devices: 118 us -> 199 us
  blocking collectives: 37.4 us -> 72 us
  other arithmetic: 4.47 us -> 10.3 us
    all_gather x0 -> x2, waiting for transfers between devices: none -> 111 us  [shards(): local_grad = jnp.sum(lax.all_gather(local_grad, 'space'), 0)]
    all_gather x0 -> x2, blocking collectives: none -> 72 us  [shards(): local_grad = jnp.sum(lax.all_gather(local_grad, 'space'), 0)]
    psum x1 -> x0, blocking collectives: 37.4 us -> none  [shards(): local_grad = lax.psum(local_grad, 'space')]
    ppermute x7, waiting for transfers between devices: 104 us -> 85.8 us  [passed_along(): return lax.ppermute(block, axis, route)]
    ppermute x2, waiting for transfers between devices: 9.74 us -> 0.61 us  [with_halo(): lax.ppermute(head, axis, [((i + 1) % count, i) for i in range(ends)])]
    reduce_sum x0 -> x4, other arithmetic: none -> 6.57 us  [shards(): local_grad = jnp.sum(lax.all_gather(local_grad, 'space'), 0)]
    psum x1 -> x0, waiting for transfers between devices: 4.18 us -> none  [shards(): local_grad = lax.psum(local_grad, 'space')]
  transfers between devices with their start and end apart: 12 -> 13, of which waited for: 7 -> 8; matrix products, arithmetic and copies ran while one was open for 7% -> 5% of each run, Pallas kernels for 0% -> 0%
where the time goes in v1:
time: 346 us; the launch traced here: 344 us
  waiting for transfers between devices  199 us (58%)
  blocking collectives  72 us (21%)
  starting transfers between devices  29.8 us (9%)
  between operations  13.8 us (4%)
  local copies, waits for them, and re-layouts  12.5 us (4%)
  other arithmetic  10.3 us (3%)
  matrix products  5.93 us (2%)
    all_gather x2, waiting for transfers between devices, shards(): local_grad = jnp.sum(lax.all_gather(local_grad, 'space'), 0)  111 us
    ppermute x7, waiting for transfers between devices, passed_along(): return lax.ppermute(block, axis, route)  85.8 us
    all_gather x2, blocking collectives, shards(): local_grad = jnp.sum(lax.all_gather(local_grad, 'space'), 0)  72 us
    ppermute x7, starting transfers between devices, passed_along(): return lax.ppermute(block, axis, route)  16.3 us
    ppermute x2, starting transfers between devices, with_halo(): lax.ppermute(tail, axis, [(i, (i + 1) % count) for i in range(ends)])  10.9 us
  transfers between devices with their start and end apart: 13, of which 8 were waited for; matrix products, arithmetic and copies ran while one was open for 5% of the time, Pallas kernels for 0%

profile of v1, /device:TPU:0, one launch (start us, length us, event | category | flops | bytes accessed | tf_op | source)
XLA Modules:
  0.0 344.0 jit_solution(8148631303813910024)
XLA Ops:
  6.5 4.9 %collective-permute-start.4 = (bf16[128,1,2,32]{0,3,2,1:T(8,128)(2,1)}, bf16[128,1,2,32]{0,3,2,1:T(8,128)(2,1)S(1)}, u32[]{:S(2)}, u32[]{:S(2)}) collective-permute-start(bf16[128,1,2,32]{0,3,2,1:T(8,128)(2,1)} %param.13), channel_id=1, source_target_pairs={{0,4},{4,8},{8,12},{12,16},{16,20},{20,24},{24,28},{1,5},{5,9},{9,... | collective-permute-start | bytes 49160 | tf_op jit(solution)/shard_map/ppermute | solution.py:50
  11.4 1.3 slice_reduce_fusion.82
  12.8 1.3 collective-permute-start.3
  14.9 4.1 %collective-permute-done.3 = bf16[64,1,4,64]{3,2,1,0:T(4,128)(2,1)S(1)} collective-permute-done((bf16[64,1,4,64]{3,2,1,0:T(4,128)(2,1)S(1)}, bf16[64,1,4,64]{3,2,1,0:T(4,128)(2,1)S(1)}, u32[]{:S(2)}, u32[]{:S(2)}) %collective-permute-start.3) | collective-permute-done | bytes 32800 | tf_op jit(solution)/shard_map/ppermute | solution.py:50
  19.9 0.9 copy-done.1
  20.9 1.0 copy.300
  21.9 1.3 collective-permute-start.5
  23.2 1.6 reduce.83
  24.8 1.3 collective-permute-start.2
  26.1 5.0 %collective-permute-start.6 = (bf16[64,1,4,64]{3,0,2,1:T(8,128)(2,1)S(1)}, bf16[64,1,4,64]{3,0,2,1:T(8,128)(2,1)S(1)}, u32[]{:S(2)}, u32[]{:S(2)}) collective-permute-start(bf16[64,1,4,64]{3,0,2,1:T(8,128)(2,1)S(1)} %copy.558), channel_id=1, source_target_pairs={{0,4},{4,8},{8,12},{12,16},{16,20},{20,24},{24,28},{1,5},{5,9},{9,... | collective-permute-start | bytes 98312 | tf_op jit(solution)/shard_map/ppermute | solution.py:50
  31.7 2.1 collective-permute-done.6
  33.9 2.1 conditional.5
  34.7 1.2 broadcast.41
  36.7 1.0 slice_reduce_fusion.83
  37.8 1.3 collective-permute-start.1
  39.1 5.0 %collective-permute-start = (bf16[4,1,8,128]{3,2,1,0:T(8,128)(2,1)S(1)}, bf16[4,1,8,128]{3,2,1,0:T(8,128)(2,1)S(1)}, u32[]{:S(2)}, u32[]{:S(2)}) collective-permute-start(bf16[4,1,8,128]{3,2,1,0:T(8,128)(2,1)S(1)} %get-tuple-element.220), channel_id=1, source_target_pairs={{0,4},{4,8},{8,12},{12,16},{16,20},{20,24},{24,28},{1,5},{5,9},{9,... | collective-permute-start | bytes 24584 | tf_op jit(solution)/shard_map/ppermute | solution.py:38
  44.1 1.6 copy.305
  45.7 1.3 collective-permute-start.7
  47.8 1.3 collective-permute-done.7
  49.2 1.3 collective-permute-start.9
  50.5 5.9 %collective-permute-start.8 = (bf16[48,1,8,128]{3,0,1,2:T(8,128)(2,1)S(1)}, bf16[48,1,8,128]{3,0,1,2:T(8,128)(2,1)S(1)}, u32[]{:S(2)}, u32[]{:S(2)}) collective-permute-start(bf16[48,1,8,128]{3,0,1,2:T(8,128)(2,1)S(1)} %get-tuple-element.218), channel_id=1, source_target_pairs={{0,4},{4,8},{8,12},{12,16},{16,20},{20,24},{24,28},{1,5},{5,9},{9,... | collective-permute-start | bytes 294920 | tf_op jit(solution)/shard_map/ppermute | solution.py:38
  57.1 1.5 collective-permute-done.8
  58.7 1.0 conditional.6
  59.7 1.3 collective-permute-start.10
  61.0 37.0 %all-gather.1 = f32[216,32,16]{1,2,0:T(8,128)S(1)} all-gather(f32[27,32,16]{1,2,0:T(8,128)} %get-tuple-element.73), channel_id=3, replica_groups=mesh['space'=8,'segment'=4] {'space'}, dimensions={0}, use_global_device_ids=true | all-gather | bytes 497664 | tf_op jit(solution)/shard_map/all_gather | solution.py:250
  98.5 77.6 %collective-permute-done.10 = bf16[16,4,8,128]{3,0,1,2:T(8,128)(2,1)S(1)} collective-permute-done((bf16[16,4,8,128]{3,0,1,2:T(8,128)(2,1)S(1)}, bf16[16,4,8,128]{3,0,1,2:T(8,128)(2,1)S(1)}, u32[]{:S(2)}, u32[]{:S(2)}) %collective-permute-start.10) | collective-permute-done | bytes 131104 | tf_op jit(solution)/shard_map/ppermute | solution.py:50
  176.1 6.0 %conditional.7 = (f32[27,16,4]{1,2,0:T(4,128)S(1)}) conditional(s32[]{:T(128)} %convert_element_type.41, () %tuple.35, (bf16[4,6,8,128]{3,2,1,0:T(8,128)(2,1)S(1)}, bf16[16,4,8,128]{3,0,1,2:T(8,128)(2,1)S(1)}) %tuple.42), branch_computations={%region_6.7_spmd, %region_7.8_spmd} | conditional | flops 14157503 | bytes 4984328 | solution.py:249
  182.1 35.0 %all-gather = f32[216,16,4]{1,2,0:T(4,128)S(1)} all-gather(f32[27,16,4]{1,2,0:T(4,128)S(1)} %get-tuple-element.234), channel_id=2, replica_groups=mesh['space'=8,'segment'=4] {'space'}, dimensions={0}, use_global_device_ids=true | all-gather | bytes 62208 | tf_op jit(solution)/shard_map/all_gather | solution.py:250
  217.7 2.5 reduce_sum.38
  220.7 110.6 %all-gather.9.cloned.1.call-done = f32[216,128,64]{1,2,0:T(8,128)} async-done(((f32[27,128,64]{1,2,0:T(8,128)}), f32[216,128,64]{1,2,0:T(8,128)}) %all-gather.9.cloned.1.call-update) | async-done | bytes 7077904 | tf_op jit(solution)/shard_map/all_gather | solution.py:250
  331.3 3.8 %reduce_sum.39 = f32[27,128,64]{1,2,0:T(8,128)S(1)} reduce(f32[8,27,128,64]{2,3,1,0:T(8,128)} %bitcast.1839, f32[]{:T(128)} %constant.64.clone.1), dimensions={0}, to_apply=%region_11.12 | reduce | flops 1548288 | bytes 7962628 | tf_op jit(solution)/shard_map/reduce_sum | solution.py:250
  336.1 1.0 select_select_fusion
  (79 shorter events, 15.6 us)
Async XLA Ops:
  6.5 211.1 %all-gather.7.cloned.1.call-start = ((), (), s32[]{:S(2)}) async-start(), calls=%async_computation | async-start | bytes 3981312 | tf_op jit(solution)/shard_map/all_gather | solution.py:250
  6.5 7.6 %collective-permute-start.4 = (bf16[128,1,2,32]{0,3,2,1:T(8,128)(2,1)}, bf16[128,1,2,32]{0,3,2,1:T(8,128)(2,1)S(1)}, u32[]{:S(2)}, u32[]{:S(2)}) collective-permute-start(bf16[128,1,2,32]{0,3,2,1:T(8,128)(2,1)} %param.13), channel_id=1, source_target_pairs={{0,4},{4,8},{8,12},{12,16},{16,20},{20,24},{24,28},{1,5},{5,9},{9,... | collective-permute-start | bytes 49160 | tf_op jit(solution)/shard_map/ppermute | solution.py:50
  12.8 6.2 %collective-permute-start.3 = (bf16[64,1,4,64]{3,2,1,0:T(4,128)(2,1)S(1)}, bf16[64,1,4,64]{3,2,1,0:T(4,128)(2,1)S(1)}, u32[]{:S(2)}, u32[]{:S(2)}) collective-permute-start(bf16[64,1,4,64]{3,2,1,0:T(4,128)(2,1)S(1)} %slice.982), channel_id=1, source_target_pairs={{4,0},{8,4},{12,8},{16,12},{20,16},{24,20},{28,24},{5,1},{9,5},{13... | collective-permute-start | bytes 98312 | tf_op jit(solution)/shard_map/ppermute | solution.py:50
  19.2 4.0 %copy-start.2 = (bf16[1,131072]{1,0:T(2,128)(2,1)S(1)}, bf16[1,131072]{1,0:T(2,128)(2,1)}, u32[]{:S(2)}) copy-start(bf16[1,131072]{1,0:T(2,128)(2,1)} %param.11) | copy-start | bytes 786436
  19.9 0.9 copy-start.1
  21.9 4.2 %collective-permute-start.5 = (bf16[64,2,4,64]{3,0,1,2:T(8,128)(2,1)S(1)}, bf16[64,2,4,64]{3,0,1,2:T(8,128)(2,1)S(1)}, u32[]{:S(2)}, u32[]{:S(2)}) collective-permute-start(bf16[64,2,4,64]{3,0,1,2:T(8,128)(2,1)S(1)} %copy.300), channel_id=1, source_target_pairs={{1,0},{2,1},{3,2},{5,4},{6,5},{7,6},{9,8},{10,9},{11,10},{13,12},{... | collective-permute-start | bytes 196616 | tf_op jit(solution)/shard_map/ppermute | solution.py:50
  24.8 6.9 %collective-permute-start.2 = (bf16[32,1,8,128]{3,2,1,0:T(8,128)(2,1)S(1)}, bf16[32,1,8,128]{3,2,1,0:T(8,128)(2,1)S(1)}, u32[]{:S(2)}, u32[]{:S(2)}) collective-permute-start(bf16[32,1,8,128]{3,2,1,0:T(8,128)(2,1)S(1)} %slice.981), channel_id=1, source_target_pairs={{4,0},{8,4},{12,8},{16,12},{20,16},{24,20},{28,24},{5,1},{9,5},{13... | collective-permute-start | bytes 196616 | tf_op jit(solution)/shard_map/ppermute | solution.py:50
  26.1 7.7 %collective-permute-start.6 = (bf16[64,1,4,64]{3,0,2,1:T(8,128)(2,1)S(1)}, bf16[64,1,4,64]{3,0,2,1:T(8,128)(2,1)S(1)}, u32[]{:S(2)}, u32[]{:S(2)}) collective-permute-start(bf16[64,1,4,64]{3,0,2,1:T(8,128)(2,1)S(1)} %copy.558), channel_id=1, source_target_pairs={{0,4},{4,8},{8,12},{12,16},{16,20},{20,24},{24,28},{1,5},{5,9},{9,... | collective-permute-start | bytes 98312 | tf_op jit(solution)/shard_map/ppermute | solution.py:50
  36.0 11.0 %copy-start.3 = (bf16[1,131072]{1,0:T(2,128)(2,1)S(1)}, bf16[1,131072]{1,0:T(2,128)(2,1)}, u32[]{:S(2)}) copy-start(bf16[1,131072]{1,0:T(2,128)(2,1)} %param.11) | copy-start | bytes 786436
  36.0 295.3 %all-gather.9.cloned.1.call-start = ((), (), s32[]{:S(2)}) async-start(), calls=%async_computation.1 | async-start | bytes 7962624 | tf_op jit(solution)/shard_map/all_gather | solution.py:250
  37.8 18.6 %collective-permute-start.1 = (bf16[4,1,8,128]{3,2,1,0:T(8,128)(2,1)S(1)}, bf16[4,1,8,128]{3,2,1,0:T(8,128)(2,1)S(1)}, u32[]{:S(2)}, u32[]{:S(2)}) collective-permute-start(bf16[4,1,8,128]{3,2,1,0:T(8,128)(2,1)S(1)} %get-tuple-element.221), channel_id=1, source_target_pairs={{4,0},{8,4},{12,8},{16,12},{20,16},{24,20},{28,24},{5,1},{9,5},{13... | collective-permute-start | bytes 24584 | tf_op jit(solution)/shard_map/ppermute | solution.py:40
  39.1 17.3 %collective-permute-start = (bf16[4,1,8,128]{3,2,1,0:T(8,128)(2,1)S(1)}, bf16[4,1,8,128]{3,2,1,0:T(8,128)(2,1)S(1)}, u32[]{:S(2)}, u32[]{:S(2)}) collective-permute-start(bf16[4,1,8,128]{3,2,1,0:T(8,128)(2,1)S(1)} %get-tuple-element.220), channel_id=1, source_target_pairs={{0,4},{4,8},{8,12},{12,16},{16,20},{20,24},{24,28},{1,5},{5,9},{9,... | collective-permute-start | bytes 24584 | tf_op jit(solution)/shard_map/ppermute | solution.py:38
  45.7 3.4 collective-permute-start.7
  49.2 7.9 %collective-permute-start.9 = (bf16[48,1,8,128]{3,0,1,2:T(8,128)(2,1)S(1)}, bf16[48,1,8,128]{3,0,1,2:T(8,128)(2,1)S(1)}, u32[]{:S(2)}, u32[]{:S(2)}) collective-permute-start(bf16[48,1,8,128]{3,0,1,2:T(8,128)(2,1)S(1)} %get-tuple-element.219), channel_id=1, source_target_pairs={{4,0},{8,4},{12,8},{16,12},{20,16},{24,20},{28,24},{5,1},{9,5},{13... | collective-permute-start | bytes 294920 | tf_op jit(solution)/shard_map/ppermute | solution.py:40
  50.5 8.1 %collective-permute-start.8 = (bf16[48,1,8,128]{3,0,1,2:T(8,128)(2,1)S(1)}, bf16[48,1,8,128]{3,0,1,2:T(8,128)(2,1)S(1)}, u32[]{:S(2)}, u32[]{:S(2)}) collective-permute-start(bf16[48,1,8,128]{3,0,1,2:T(8,128)(2,1)S(1)} %get-tuple-element.218), channel_id=1, source_target_pairs={{0,4},{4,8},{8,12},{12,16},{16,20},{20,24},{24,28},{1,5},{5,9},{9,... | collective-permute-start | bytes 294920 | tf_op jit(solution)/shard_map/ppermute | solution.py:38
  59.7 116.4 %collective-permute-start.10 = (bf16[16,4,8,128]{3,0,1,2:T(8,128)(2,1)S(1)}, bf16[16,4,8,128]{3,0,1,2:T(8,128)(2,1)S(1)}, u32[]{:S(2)}, u32[]{:S(2)}) collective-permute-start(bf16[16,4,8,128]{3,0,1,2:T(8,128)(2,1)S(1)} %copy.308), channel_id=1, source_target_pairs={{1,0},{2,1},{3,2},{5,4},{6,5},{7,6},{9,8},{10,9},{11,10},{13,12},{... | collective-permute-start | bytes 393224 | tf_op jit(solution)/shard_map/ppermute | solution.py:50
Sparse Core Ops, SparseCore 0:
  36.1 158.7 all-gather.6
  197.1 134.1 all-gather.8
